TPU v7x, 32 devices: a whole 2x2x4 slice. The times are simulated.
32 devices in a mesh: tile: 8 (over y, x, core), depth: 4 (over z).
Axes of the slice: x: 2, y: 2, z: 4, core: 2. Of those that a mesh axis runs over, the one named last changes fastest.
Arguments:
- patches: float32 [512, 256, 256], P('tile', 'depth'), may hold values from -6 to 6
- patch_owner: int32 [512, 1], P('tile'), may hold values from 0 to 7; in each aligned block of 64 rows (0 to 63, 64 to 127, ...) at most 8 rows name the same one
- patch_level: int32 [512], P('tile'), may hold values from 0 to 63
- phases: float32 [512, 256, 256], P('tile', None, 'depth'), may hold values from -3.140625 to 3.140625
Outputs:
- intensity: float32 [512, 256, 256], P('tile', 'depth')
Inputs may be any that keep to these rules, and one draw needn't show every extreme that they name: `patch_owner`: among the 64 patches of one index of tile, at most 8 have the same owner.
All inputs are finite; a program needn't handle non-finite values.
Results may differ from a plain program's by a relative error of at most 0.00017.
Values sent between devices are 32-bit elements; how exact they have to be, the bound alone decides.
No kernel may reach another device: no remote copies, remote signals or barrier semaphores. Data moves between devices by JAX's collectives and lax.ppermute only.
A program may use at most 128 MiB of HBM per device.

v0:
```python
import functools
import math

import jax
import jax.numpy as jnp
import numpy as np
from jax import lax
from jax.experimental import pallas as pl
from jax.experimental.pallas import tpu as pltpu
from jax.sharding import PartitionSpec as P


CAP = 8
CHUNKS = 2
TOGETHER = 2


def split(values):
    high = values.astype(jnp.bfloat16)
    low = (values - high.astype(jnp.float32)).astype(jnp.bfloat16)
    return high, low


def tables(extent):
    index = np.arange(extent)
    angles = (index[:, None] * index[None, :] % extent) * (2.0 * math.pi / extent)
    parts = []
    for table in (np.cos(angles), np.sin(angles)):
        table = table.astype(np.float32)
        high = table.astype(jnp.bfloat16)
        parts += [high, (table - high.astype(np.float32)).astype(jnp.bfloat16)]
    return np.stack(parts)


def sincos(angle):
    half = angle * 0.5
    square = half * half
    sine = jnp.float32(-1.0 / math.factorial(11))
    for power, sign in ((9, 1.0), (7, -1.0), (5, 1.0), (3, -1.0), (1, 1.0)):
        sine = sine * square + jnp.float32(sign / math.factorial(power))
    sine = sine * half
    cosine = jnp.float32(1.0 / math.factorial(12))
    for power, sign in ((10, -1.0), (8, 1.0), (6, -1.0), (4, 1.0), (2, -1.0), (0, 1.0)):
        cosine = cosine * square + jnp.float32(sign / math.factorial(power))
    return 2.0 * sine * cosine, 1.0 - 2.0 * sine * sine


def product(left, right, contract):
    dims = (contract, ((), ()))
    dot = functools.partial(
        lax.dot_general, dimension_numbers=dims, preferred_element_type=jnp.float32
    )
    return dot(left[0], right[0]) + (dot(left[0], right[1]) + dot(left[1], right[0]))


NN = ((1,), (0,))
NT = ((1,), (1,))


def partner(step):
    return lax.bitwise_xor(lax.axis_index("depth"), step)


def rows_with(step, rows):
    return pl.ds(pl.multiple_of(partner(step) * rows, rows), rows)


def refocus_kernel(pieces, table_ref, *refs):
    field_refs, phase_refs = refs[:pieces], refs[pieces : 2 * pieces]
    out_refs = refs[2 * pieces : 3 * pieces]
    left_ref, right_ref, *whole_refs = refs[3 * pieces :]
    extent = table_ref.shape[1]

    @pl.when(pl.program_id(0) == 0)
    def _():
        for part in range(2):
            cosine, sine = table_ref[part], table_ref[2 + part]
            left_ref[part, :extent, :extent] = cosine
            left_ref[part, :extent, extent:] = -sine
            left_ref[part, extent:, :extent] = sine
            left_ref[part, extent:, extent:] = cosine
            right_ref[part, :extent, :extent] = cosine
            right_ref[part, :extent, extent:] = sine
            right_ref[part, extent:, :extent] = -sine
            right_ref[part, extent:, extent:] = cosine

    left = (left_ref[0], left_ref[1])
    right = (right_ref[0], right_ref[1])

    def one(at, whole_ref):
        def whole(refs):
            if pieces == 1:
                return refs[0][:, at].reshape(extent, extent)
            for step, ref in enumerate(refs):
                whole_ref[rows_with(step, ref.shape[1]), :] = ref[at]
            return whole_ref[...]

        half_turned = product(
            (left_ref[0, :, :extent], left_ref[1, :, :extent]), split(whole(field_refs)), NT
        )
        half_turned = jnp.concatenate([half_turned[:extent], half_turned[extent:]], axis=1)
        spectrum = product(split(half_turned), right, NN)
        spec_real, spec_negated = spectrum[:, :extent], spectrum[:, extent:]
        sine, cosine = sincos(whole(phase_refs))
        prop_real = spec_real * cosine + spec_negated * sine
        prop_imag = spec_real * sine - spec_negated * cosine
        propagated = jnp.concatenate([prop_real, prop_imag], axis=1)
        back = product(left, split(propagated), NT)
        back = jnp.concatenate([back[:extent], back[extent:]], axis=1)
        field = product(split(back), right, NN)
        field_real, field_imag = field[:, :extent], field[:, extent:]
        power = field_real * field_real + field_imag * field_imag
        intensity = power * (1.0 / float(extent) ** 4)
        if pieces == 1:
            shape = out_refs[0].shape
            out_refs[0][:, at] = intensity.reshape(shape[:1] + shape[2:])
        else:
            whole_ref[...] = intensity
            for step, ref in enumerate(out_refs):
                ref[at] = whole_ref[rows_with(step, ref.shape[1]), :]

    for at, whole_ref in enumerate(whole_refs):
        one(at, whole_ref)


def refocus(fields, phases, chunk=0):
    pieces, extent = len(fields), fields[0].shape[-1]
    if pieces == 1:
        slots = fields[0].shape[1]
        together = math.gcd(slots, TOGETHER)

        def spec(array):
            block = array.shape[:1] + (together,) + array.shape[2:]
            return pl.BlockSpec(block, lambda i: (0, i, 0, 0))
    else:
        slots = phases[0].shape[0]
        together = math.gcd(slots, TOGETHER)

        def spec(array):
            first = chunk * slots // together if array.shape[0] > slots else 0
            return pl.BlockSpec((together,) + array.shape[1:], lambda i: (first + i, 0, 0))

    shape = fields[0].shape if pieces == 1 else (slots,) + fields[0].shape[1:]
    outs = [jax.ShapeDtypeStruct(shape, jnp.float32)] * pieces
    return pl.pallas_call(
        functools.partial(refocus_kernel, pieces),
        grid=(slots // together,),
        in_specs=[pl.BlockSpec((4, extent, extent), lambda i: (0, 0, 0))]
        + [spec(array) for array in [*fields, *phases]],
        out_specs=[spec(array) for array in outs],
        out_shape=outs,
        scratch_shapes=[pltpu.VMEM((2, 2 * extent, 2 * extent), jnp.bfloat16)] * 2
        + [pltpu.VMEM((extent, extent), jnp.float32)] * together,
        name="refocus",
    )(jnp.asarray(tables(extent)), *fields, *phases)


def move_kernel(scatter, filled, *refs):
    index_ref, source_ref, out_ref, held, come, gone = refs[0], refs[1], *refs[-4:]
    count = held.shape[0]

    def guarded(place, act):
        if filled:
            act()
        else:
            pl.when(place >= 0)(act)

    def each(act):
        def step(i, carry):
            guarded(index_ref[i], lambda: act(i))
            return carry

        lax.fori_loop(0, count, step, 0)

    def fetch(i):
        block = source_ref.at[i if scatter else index_ref[i]]
        return pltpu.make_async_copy(block, held.at[i], come.at[i])

    def store(i):
        block = out_ref.at[index_ref[i] if scatter else i]
        return pltpu.make_async_copy(held.at[i], block, gone.at[i])

    def pass_on(i):
        fetch(i).wait()
        store(i).start()

    each(lambda i: fetch(i).start())
    each(pass_on)
    each(lambda i: store(i).wait())


def move(index, source, out_shape, scatter, filled, into=None):
    count = index.shape[0]
    anywhere = pl.BlockSpec(memory_space=pl.ANY)
    operands = (source,) if into is None else (source, into)
    return pl.pallas_call(
        functools.partial(move_kernel, scatter, filled),
        grid_spec=pltpu.PrefetchScalarGridSpec(
            num_scalar_prefetch=1,
            in_specs=[anywhere] * len(operands),
            out_specs=anywhere,
            scratch_shapes=[
                pltpu.VMEM((count,) + source.shape[1:], source.dtype),
                pltpu.SemaphoreType.DMA((count,)),
                pltpu.SemaphoreType.DMA((count,)),
            ],
        ),
        out_shape=jax.ShapeDtypeStruct(out_shape, source.dtype),
        input_output_aliases={} if into is None else {2: 0},
        name="scatter_blocks" if scatter else "gather_blocks",
    )(index, *operands)


def loop(count, act):
    def step(i, carry):
        act(i)
        return carry

    lax.fori_loop(0, count, step, 0)


ANYWHERE = pl.BlockSpec(memory_space=pl.ANY)
SCALARS = pl.BlockSpec(memory_space=pltpu.SMEM)
LOCAL = pl.BlockSpec(memory_space=pltpu.VMEM)


def pieces_kernel(steps, patches_ref, *refs):
    out_refs, sems = refs[:-1], refs[-1]

    def copy(at, step):
        size = out_refs[at].shape[0]
        first = pl.multiple_of(partner(step) * size, size)
        return pltpu.make_async_copy(
            patches_ref.at[pl.ds(first, size)], out_refs[at], sems.at[at]
        )

    for at, step in enumerate(steps):
        copy(at, step).start()
    for at, step in enumerate(steps):
        copy(at, step).wait()


def pieces_of(patches, parts, steps, stay):
    shape = (patches.shape[0] // parts,) + patches.shape[1:]
    made = pltpu.VMEM if stay else jax.ShapeDtypeStruct
    return pl.pallas_call(
        functools.partial(pieces_kernel, steps),
        in_specs=[ANYWHERE],
        out_specs=[LOCAL] * len(steps),
        out_shape=[made(shape, patches.dtype)] * len(steps),
        scratch_shapes=[pltpu.SemaphoreType.DMA((len(steps),))],
        name="pieces",
    )(patches)


def table_kernel(filled, owner_ref, level_ref, slot_ref, wanted_ref, taken):
    owners, slot_count = taken.shape[0], wanted_ref.shape[0]

    def clear(i):
        taken[i] = 0

    loop(owners, clear)
    if not filled:

        def empty(i):
            wanted_ref[i] = 0

        loop(slot_count, empty)

    def place(i):
        owner = owner_ref[i]
        rank = taken[owner]
        taken[owner] = rank + 1
        slot = owner * (slot_count // owners) + rank
        slot_ref[i] = slot
        wanted_ref[slot] = level_ref[i]

    loop(owner_ref.shape[0], place)


def slot_table(owner, level, owners, slot_count):
    count = owner.shape[0]
    return pl.pallas_call(
        functools.partial(table_kernel, count == slot_count),
        in_specs=[SCALARS, SCALARS],
        out_specs=[SCALARS, SCALARS],
        out_shape=[
            jax.ShapeDtypeStruct((count,), jnp.int32),
            jax.ShapeDtypeStruct((slot_count,), jnp.int32),
        ],
        scratch_shapes=[pltpu.SMEM((owners,), jnp.int32)],
        name="slot_table",
    )(owner, level)


def order_kernel(chunk, chunks, slot_ref, source_ref, *refs):
    out_refs, (held, come, gone) = refs[:-3], refs[-3:]
    parts, size = held.shape[:2]

    def fetch(step):
        def one(i):
            slot = slot_ref[(partner(step) * chunks + chunk) * size + i]
            pltpu.make_async_copy(
                source_ref.at[slot], held.at[step, i], come.at[step, i]
            ).start()

        return one

    def pass_on(step):
        def one(i):
            pltpu.make_async_copy(source_ref.at[0], held.at[step, i], come.at[step, i]).wait()

        return one

    def store(step):
        return pltpu.make_async_copy(held.at[step], out_refs[step], gone.at[step])

    for step in range(parts):
        loop(size, fetch(step))
    for step in range(parts):
        loop(size, pass_on(step))
        store(step).start()
    for step in range(parts):
        store(step).wait()


def in_order(slots, source, parts, chunk, chunks):
    block = source.shape[1:]
    size = slots.shape[0] // (parts * chunks)
    return pl.pallas_call(
        functools.partial(order_kernel, chunk, chunks),
        in_specs=[SCALARS, ANYWHERE],
        out_specs=[ANYWHERE] * parts,
        out_shape=[jax.ShapeDtypeStruct((size,) + block, source.dtype)] * parts,
        scratch_shapes=[
            pltpu.VMEM((parts, size) + block, source.dtype),
            pltpu.SemaphoreType.DMA((parts, size)),
            pltpu.SemaphoreType.DMA((parts,)),
        ],
        name="in_order",
    )(slots, source)


def store_kernel(chunk, chunks, steps, *refs):
    source_refs, out_ref, gone = refs[: len(steps)], refs[-2], refs[-1]

    def copy(at, step):
        size = source_refs[at].shape[0]
        first = pl.multiple_of((partner(step) * chunks + chunk) * size, size)
        return pltpu.make_async_copy(source_refs[at], out_ref.at[pl.ds(first, size)], gone.at[at])

    for at, step in enumerate(steps):
        copy(at, step).start()
    for at, step in enumerate(steps):
        copy(at, step).wait()


def store(sources, into, out_shape, chunk, chunks, steps):
    sources = [pltpu.with_memory_space_constraint(source, pltpu.VMEM) for source in sources]
    operands = sources if into is None else sources + [into]
    return pl.pallas_call(
        functools.partial(store_kernel, chunk, chunks, steps),
        in_specs=[LOCAL] * len(sources) + [ANYWHERE] * (into is not None),
        out_specs=ANYWHERE,
        out_shape=jax.ShapeDtypeStruct(out_shape, jnp.float32),
        scratch_shapes=[pltpu.SemaphoreType.DMA((len(steps),))],
        input_output_aliases={} if into is None else {len(sources): 0},
        name="store",
    )(*operands)


def swap(arrays):
    parts = len(arrays)
    swapped = list(arrays)
    for step in range(parts - 1, 0, -1):
        swapped[step] = lax.ppermute(
            arrays[step], "depth", [(part, part ^ step) for part in range(parts)]
        )
    return swapped


def exchange(values, axes):
    return lax.all_to_all(values, axes, split_axis=0, concat_axis=0, tiled=True)


def by_patch(patches, patch_owner, patch_level, phases):
    owners, parts = lax.axis_size("tile"), lax.axis_size("depth")
    slot_count = owners * CAP
    (longest,) = pieces_of(patches, parts, (parts - 1,), True)
    slots, wanted = slot_table(patch_owner[:, 0], patch_level, owners, slot_count)
    wanted = exchange(wanted.reshape(owners, CAP), "tile").reshape(-1)
    rest = pieces_of(patches, parts, tuple(range(parts - 1)), False)
    fields = swap([*rest, longest])
    picked = move(wanted, phases, (slot_count,) + phases.shape[1:], False, True)
    arrived = exchange(picked, "tile")
    result = None
    for chunk in range(CHUNKS):
        chosen = in_order(slots, arrived, parts, chunk, CHUNKS)
        chosen = swap(chosen)
        local = refocus(fields, chosen, chunk)
        backs = swap(local)
        every = tuple(range(parts))
        last = chunk == CHUNKS - 1
        for steps in [(step,) for step in (*every[:2], *every[:1:-1])] if last else (every,):
            sources = [backs[step] for step in steps]
            result = store(sources, result, patches.shape, chunk, CHUNKS, steps)
    return result


def by_owner(patches, patch_owner, patch_level, phases):
    patch_count, row_count, extent = patches.shape
    owners, parts = lax.axis_size("tile"), lax.axis_size("depth")
    slot_count = owners * CAP
    filled = slot_count == patch_count
    owner = patch_owner[:, 0]
    numbers = jnp.arange(patch_count, dtype=jnp.int32)
    rank = jnp.sum(
        (owner[:, None] == owner[None, :]) & (numbers[None, :] < numbers[:, None]),
        axis=1,
        dtype=jnp.int32,
    )
    slot_hot = jnp.arange(slot_count, dtype=jnp.int32)[:, None] == (owner * CAP + rank)[None, :]
    wanted = jnp.sum(jnp.where(slot_hot, patch_level[None, :], 0), axis=1, dtype=jnp.int32)
    order = jnp.sum(jnp.where(slot_hot, numbers[None, :] + 1, 0), axis=1, dtype=jnp.int32) - 1
    wanted = exchange(wanted.reshape(owners, CAP), "tile").reshape(-1)
    field = exchange(move(order, patches, (slot_count,) + patches.shape[1:], False, filled), "depth")
    picked = move(wanted, phases, (slot_count,) + phases.shape[1:], False, True)
    phase = exchange(exchange(picked, "tile"), "depth")
    (local,) = refocus(
        [field.reshape(parts, -1, row_count, extent)],
        [phase.reshape((parts, -1) + phases.shape[1:])],
    )
    back = exchange(local.reshape(-1, row_count, extent), "depth")
    return move(order, back, patches.shape, True, filled)


def in_shares(parts):
    return parts in (2, 4)


def on_device(patches, patch_owner, patch_level, phases):
    turned = jnp.transpose(phases, (0, 2, 1))
    plan = by_patch if in_shares(lax.axis_size("depth")) else by_owner
    return plan(patches, patch_owner, patch_level, turned)


def solution(mesh):
    return jax.shard_map(
        on_device,
        mesh=mesh,
        in_specs=(P("tile", "depth", None), P("tile", None), P("tile"), P("tile", None, "depth")),
        out_specs=P("tile", "depth", None),
        check_vma=False,
    )
```

profile of v0, /device:TPU:0, one launch (start us, length us, event | category | flops | bytes accessed | tf_op | source)
XLA Modules:
  0.0 307.7 jit_solution(7578029229180911396)
XLA Ops:
  0.0 1.8 slot_table.1
  1.8 0.7 all_to_all.9
  2.5 9.7 %all_to_all.14 = s32[8,1,8]{2,1,0:T(1,128)S(1)} all-to-all(s32[8,1,8]{2,1,0:T(1,128)S(1)} %bitcast.4), channel_id=1, replica_groups=mesh['tile'=8,'depth'=4] {'tile'}, dimensions={0} | all-to-all | bytes 512 | tf_op jit(solution)/shard_map/all_to_all | solution.py:383
  12.2 0.5 broadcast.3
  12.7 0.7 reduce.3
  13.4 0.7 reshape.8.refs_0_
  14.1 5.8 %gather_blocks.1 = f32[64,64,256]{2,1,0:T(8,128)} custom-call(s32[64]{0:T(128)} %reshape.8.refs_0_, f32[64,64,256]{2,1,0:T(8,128)} %bitcast.3), custom_call_target="tpu_custom_call" | custom-call | tf_op jit(solution)/shard_map/gather_blocks/pallas_call | solution.py:196
  19.9 4.6 %all-to-all-start.1 = ((f32[64,64,256]{2,1,0:T(8,128)}), f32[64,64,256]{2,1,0:T(8,128)}, u32[]{:S(2)}, u32[]{:S(2)}) async-start(f32[64,64,256]{2,1,0:T(8,128)} %gather_blocks.1), calls=%async_computation.1 | async-start | bytes 8388608 | tf_op jit(solution)/shard_map/all_to_all | solution.py:383
  24.5 1.2 pieces.3
  25.7 3.7 %collective-permute-start.2 = (f32[16,64,256]{2,1,0:T(8,128)S(1)}, f32[16,64,256]{2,1,0:T(8,128)S(1)}, u32[]{:S(2)}, u32[]{:S(2)}) collective-permute-start(f32[16,64,256]{2,1,0:T(8,128)S(1)} %pieces.3), channel_id=1, source_target_pairs={{0,3},{1,2},{2,1},{3,0},{4,7},{5,6},{6,5},{7,4},{8,11},{9,10},{10,... | collective-permute-start | bytes 3145736 | tf_op jit(solution)/shard_map/ppermute | solution.py:376
  29.4 3.7 %pieces.2 = (f32[16,64,256]{2,1,0:T(8,128)}, f32[16,64,256]{2,1,0:T(8,128)}, f32[16,64,256]{2,1,0:T(8,128)}) custom-call(f32[64,64,256]{2,1,0:T(8,128)} %patches_ref.3), custom_call_target="tpu_custom_call" | custom-call | tf_op jit(solution)/shard_map/pieces/pallas_call | solution.py:246
  33.1 0.1 collective-permute-start
  33.1 0.8 collective-permute-start.1
  33.9 39.6 %all-to-all-done.1.source_ref = f32[64,64,256]{2,1,0:T(8,128)} async-done(((f32[64,64,256]{2,1,0:T(8,128)}), f32[64,64,256]{2,1,0:T(8,128)}, u32[]{:S(2)}, u32[]{:S(2)}) %all-to-all-start.1) | async-done | bytes 4194336 | tf_op jit(solution)/shard_map/all_to_all | solution.py:383
  73.6 3.4 %in_order.3 = (f32[8,64,256]{2,1,0:T(8,128)}, f32[8,64,256]{2,1,0:T(8,128)}, f32[8,64,256]{2,1,0:T(8,128)}, f32[8,64,256]{2,1,0:T(8,128)}) custom-call(s32[64]{0:T(128)} %get-tuple-element.29.slot_ref, f32[64,64,256]{2,1,0:T(8,128)} %all-to-all-done.1.source_ref), custom_call_target="tpu_custom_call" | custom-call | tf_op jit(solution)/shard_map/in_order/pallas_call | solution.py:330
  77.0 1.6 collective-permute-start.9
  78.6 2.6 collective-permute-start.10
  81.2 0.0 collective-permute-done.2.refs_3_
  81.2 0.2 collective-permute-start.11
  81.4 3.4 %in_order.2 = (f32[8,64,256]{2,1,0:T(8,128)}, f32[8,64,256]{2,1,0:T(8,128)}, f32[8,64,256]{2,1,0:T(8,128)}, f32[8,64,256]{2,1,0:T(8,128)}) custom-call(s32[64]{0:T(128)} %get-tuple-element.29.slot_ref, f32[64,64,256]{2,1,0:T(8,128)} %all-to-all-done.1.source_ref), custom_call_target="tpu_custom_call" | custom-call | tf_op jit(solution)/shard_map/in_order/pallas_call | solution.py:330
  84.9 0.0 collective-permute-done.refs_1_
  84.9 0.0 copy-start.3
  84.9 0.7 collective-permute-start.3
  85.7 57.2 %collective-permute-done.1.refs_2_ = f32[16,64,256]{2,1,0:T(8,128)} collective-permute-done((f32[16,64,256]{2,1,0:T(8,128)}, f32[16,64,256]{2,1,0:T(8,128)}, u32[]{:S(2)}, u32[]{:S(2)}) %collective-permute-start.1) | collective-permute-done | bytes 1048608 | tf_op jit(solution)/shard_map/ppermute | solution.py:376
  142.9 0.0 collective-permute-start.4
  142.9 0.0 collective-permute-done.9.refs_5_
  142.9 2.5 collective-permute-start.5
  145.3 31.2 %collective-permute-done.10.refs_6_ = f32[8,64,256]{2,1,0:T(8,128)} collective-permute-done((f32[8,64,256]{2,1,0:T(8,128)}, f32[8,64,256]{2,1,0:T(8,128)}, u32[]{:S(2)}, u32[]{:S(2)}) %collective-permute-start.10) | collective-permute-done | bytes 524320 | tf_op jit(solution)/shard_map/ppermute | solution.py:376
  176.6 0.0 collective-permute-done.11.refs_7_
  176.6 0.8 copy-done.4
  177.4 24.3 %refocus.3 = (f32[8,64,256]{2,1,0:T(8,128)}, f32[8,64,256]{2,1,0:T(8,128)}, f32[8,64,256]{2,1,0:T(8,128)}, f32[8,64,256]{2,1,0:T(8,128)}) custom-call(bf16[4,256,256]{2,1,0:T(8,128)(2,1)} %constant.2.clone.table_ref, f32[16,64,256]{2,1,0:T(8,128)} %get-tuple-element.26.refs_0_, f32[16,64,256]{2,1,0:T(8,128)} %copy-done.3, ...), custom_call_target="tpu_custom_call" | custom-call | tf_op jit(solution)/shard_map/refocus/pallas_call | solution.py:145
  201.7 11.8 %collective-permute-start.12 = (f32[8,64,256]{2,1,0:T(8,128)}, f32[8,64,256]{2,1,0:T(8,128)S(1)}, u32[]{:S(2)}, u32[]{:S(2)}) collective-permute-start(f32[8,64,256]{2,1,0:T(8,128)} %get-tuple-element.44), channel_id=1, source_target_pairs={{0,1},{1,0},{2,3},{3,2},{4,5},{5,4},{6,7},{7,6},{8,9},{9,8},{10,11... | collective-permute-start | bytes 1572872 | tf_op jit(solution)/shard_map/ppermute | solution.py:376
  213.4 1.1 collective-permute-start.13
  214.5 0.0 collective-permute-done.3.refs_5_
  214.5 1.4 collective-permute-start.14
  215.9 24.4 %refocus.2 = (f32[8,64,256]{2,1,0:T(8,128)}, f32[8,64,256]{2,1,0:T(8,128)}, f32[8,64,256]{2,1,0:T(8,128)}, f32[8,64,256]{2,1,0:T(8,128)}) custom-call(bf16[4,256,256]{2,1,0:T(8,128)(2,1)} %constant.2.clone.table_ref, f32[16,64,256]{2,1,0:T(8,128)} %get-tuple-element.26.refs_0_, f32[16,64,256]{2,1,0:T(8,128)} %copy-done.3, ...), custom_call_target="tpu_custom_call" | custom-call | tf_op jit(solution)/shard_map/refocus/pallas_call | solution.py:145
  240.3 1.1 collective-permute-start.8
  241.4 2.5 collective-permute-start.7
  243.8 8.0 %collective-permute-done.13.refs_2_ = f32[8,64,256]{2,1,0:T(8,128)S(1)} collective-permute-done((f32[8,64,256]{2,1,0:T(8,128)}, f32[8,64,256]{2,1,0:T(8,128)S(1)}, u32[]{:S(2)}, u32[]{:S(2)}) %collective-permute-start.13) | collective-permute-done | bytes 524320 | tf_op jit(solution)/shard_map/ppermute | solution.py:376
  251.8 0.0 collective-permute-done.14.refs_3_
  251.8 1.3 store.5.refs_1_
  253.2 0.8 store.6.refs_1_
  254.0 18.2 %collective-permute-done.8.refs_0_ = f32[8,64,256]{2,1,0:T(8,128)} collective-permute-done((f32[8,64,256]{2,1,0:T(8,128)}, f32[8,64,256]{2,1,0:T(8,128)}, u32[]{:S(2)}, u32[]{:S(2)}) %collective-permute-start.8) | collective-permute-done | bytes 524320 | tf_op jit(solution)/shard_map/ppermute | solution.py:376
  272.2 1.8 store.7.refs_1_
  274.1 0.0 collective-permute-done.7.refs_0_
  274.1 0.8 store.8.refs_1_
  274.9 30.9 %collective-permute-done.6.refs_0_ = f32[8,64,256]{2,1,0:T(8,128)} collective-permute-done((f32[8,64,256]{2,1,0:T(8,128)}, f32[8,64,256]{2,1,0:T(8,128)}, u32[]{:S(2)}, u32[]{:S(2)}) %collective-permute-start.6) | collective-permute-done | bytes 524320 | tf_op jit(solution)/shard_map/ppermute | solution.py:376
  305.8 1.8 store.9
  (12 shorter events, 0.0 us)
Async XLA Ops:
  19.9 53.7 %all-to-all-start.1 = ((f32[64,64,256]{2,1,0:T(8,128)}), f32[64,64,256]{2,1,0:T(8,128)}, u32[]{:S(2)}, u32[]{:S(2)}) async-start(f32[64,64,256]{2,1,0:T(8,128)} %gather_blocks.1), calls=%async_computation.1 | async-start | bytes 8388608 | tf_op jit(solution)/shard_map/all_to_all | solution.py:383
  25.7 55.5 %collective-permute-start.2 = (f32[16,64,256]{2,1,0:T(8,128)S(1)}, f32[16,64,256]{2,1,0:T(8,128)S(1)}, u32[]{:S(2)}, u32[]{:S(2)}) collective-permute-start(f32[16,64,256]{2,1,0:T(8,128)S(1)} %pieces.3), channel_id=1, source_target_pairs={{0,3},{1,2},{2,1},{3,0},{4,7},{5,6},{6,5},{7,4},{8,11},{9,10},{10,... | collective-permute-start | bytes 3145736 | tf_op jit(solution)/shard_map/ppermute | solution.py:376
  33.1 51.8 %collective-permute-start = (f32[16,64,256]{2,1,0:T(8,128)}, f32[16,64,256]{2,1,0:T(8,128)S(1)}, u32[]{:S(2)}, u32[]{:S(2)}) collective-permute-start(f32[16,64,256]{2,1,0:T(8,128)} %get-tuple-element.27), channel_id=1, source_target_pairs={{0,1},{1,0},{2,3},{3,2},{4,5},{5,4},{6,7},{7,6},{8,9},{9,8},{10,11... | collective-permute-start | bytes 3145736 | tf_op jit(solution)/shard_map/ppermute | solution.py:376
  33.1 109.7 %collective-permute-start.1 = (f32[16,64,256]{2,1,0:T(8,128)}, f32[16,64,256]{2,1,0:T(8,128)}, u32[]{:S(2)}, u32[]{:S(2)}) collective-permute-start(f32[16,64,256]{2,1,0:T(8,128)} %get-tuple-element.28), channel_id=1, source_target_pairs={{0,2},{1,3},{2,0},{3,1},{4,6},{5,7},{6,4},{7,5},{8,10},{9,11},{10,... | collective-permute-start | bytes 3145736 | tf_op jit(solution)/shard_map/ppermute | solution.py:376
  77.0 65.9 %collective-permute-start.9 = (f32[8,64,256]{2,1,0:T(8,128)}, f32[8,64,256]{2,1,0:T(8,128)}, u32[]{:S(2)}, u32[]{:S(2)}) collective-permute-start(f32[8,64,256]{2,1,0:T(8,128)} %get-tuple-element.40), channel_id=1, source_target_pairs={{0,1},{1,0},{2,3},{3,2},{4,5},{5,4},{6,7},{7,6},{8,9},{9,8},{10,11... | collective-permute-start | bytes 1572872 | tf_op jit(solution)/shard_map/ppermute | solution.py:376
  78.6 97.9 %collective-permute-start.10 = (f32[8,64,256]{2,1,0:T(8,128)}, f32[8,64,256]{2,1,0:T(8,128)}, u32[]{:S(2)}, u32[]{:S(2)}) collective-permute-start(f32[8,64,256]{2,1,0:T(8,128)} %get-tuple-element.41), channel_id=1, source_target_pairs={{0,2},{1,3},{2,0},{3,1},{4,6},{5,7},{6,4},{7,5},{8,10},{9,11},{10,... | collective-permute-start | bytes 1572872 | tf_op jit(solution)/shard_map/ppermute | solution.py:376
  81.2 95.3 %copy-start.2 = (f32[16,64,256]{2,1,0:T(8,128)}, f32[16,64,256]{2,1,0:T(8,128)S(1)}, u32[]{:S(2)}) copy-start(f32[16,64,256]{2,1,0:T(8,128)S(1)} %collective-permute-done.2.refs_3_) | copy-start | bytes 3145732
  81.2 95.3 %collective-permute-start.11 = (f32[8,64,256]{2,1,0:T(8,128)}, f32[8,64,256]{2,1,0:T(8,128)S(1)}, u32[]{:S(2)}, u32[]{:S(2)}) collective-permute-start(f32[8,64,256]{2,1,0:T(8,128)} %get-tuple-element.42), channel_id=1, source_target_pairs={{0,3},{1,2},{2,1},{3,0},{4,7},{5,6},{6,5},{7,4},{8,11},{9,10},{10,... | collective-permute-start | bytes 1572872 | tf_op jit(solution)/shard_map/ppermute | solution.py:376
  84.9 91.7 %copy-start.3 = (f32[16,64,256]{2,1,0:T(8,128)}, f32[16,64,256]{2,1,0:T(8,128)S(1)}, u32[]{:S(2)}) copy-start(f32[16,64,256]{2,1,0:T(8,128)S(1)} %collective-permute-done.refs_1_) | copy-start | bytes 3145732
  84.9 129.6 %collective-permute-start.3 = (f32[8,64,256]{2,1,0:T(8,128)}, f32[8,64,256]{2,1,0:T(8,128)}, u32[]{:S(2)}, u32[]{:S(2)}) collective-permute-start(f32[8,64,256]{2,1,0:T(8,128)} %get-tuple-element.32), channel_id=1, source_target_pairs={{0,1},{1,0},{2,3},{3,2},{4,5},{5,4},{6,7},{7,6},{8,9},{9,8},{10,11... | collective-permute-start | bytes 1572872 | tf_op jit(solution)/shard_map/ppermute | solution.py:376
  142.9 73.1 %collective-permute-start.4 = (f32[8,64,256]{2,1,0:T(8,128)}, f32[8,64,256]{2,1,0:T(8,128)}, u32[]{:S(2)}, u32[]{:S(2)}) collective-permute-start(f32[8,64,256]{2,1,0:T(8,128)} %get-tuple-element.33), channel_id=1, source_target_pairs={{0,2},{1,3},{2,0},{3,1},{4,6},{5,7},{6,4},{7,5},{8,10},{9,11},{10,... | collective-permute-start | bytes 1572872 | tf_op jit(solution)/shard_map/ppermute | solution.py:376
  142.9 73.1 %collective-permute-start.5 = (f32[8,64,256]{2,1,0:T(8,128)}, f32[8,64,256]{2,1,0:T(8,128)}, u32[]{:S(2)}, u32[]{:S(2)}) collective-permute-start(f32[8,64,256]{2,1,0:T(8,128)} %get-tuple-element.34), channel_id=1, source_target_pairs={{0,3},{1,2},{2,1},{3,0},{4,7},{5,6},{6,5},{7,4},{8,11},{9,10},{10,... | collective-permute-start | bytes 1572872 | tf_op jit(solution)/shard_map/ppermute | solution.py:376
  176.6 0.8 copy-start.4
  201.7 50.2 %copy-start = (f32[8,64,256]{2,1,0:T(8,128)S(1)}, f32[8,64,256]{2,1,0:T(8,128)}, u32[]{:S(2)}) copy-start(f32[8,64,256]{2,1,0:T(8,128)} %get-tuple-element.43.refs_0_) | copy-start | bytes 1572868
  201.7 42.2 %collective-permute-start.12 = (f32[8,64,256]{2,1,0:T(8,128)}, f32[8,64,256]{2,1,0:T(8,128)S(1)}, u32[]{:S(2)}, u32[]{:S(2)}) collective-permute-start(f32[8,64,256]{2,1,0:T(8,128)} %get-tuple-element.44), channel_id=1, source_target_pairs={{0,1},{1,0},{2,3},{3,2},{4,5},{5,4},{6,7},{7,6},{8,9},{9,8},{10,11... | collective-permute-start | bytes 1572872 | tf_op jit(solution)/shard_map/ppermute | solution.py:376
  213.4 38.4 %collective-permute-start.13 = (f32[8,64,256]{2,1,0:T(8,128)}, f32[8,64,256]{2,1,0:T(8,128)S(1)}, u32[]{:S(2)}, u32[]{:S(2)}) collective-permute-start(f32[8,64,256]{2,1,0:T(8,128)} %get-tuple-element.45), channel_id=1, source_target_pairs={{0,2},{1,3},{2,0},{3,1},{4,6},{5,7},{6,4},{7,5},{8,10},{9,11},{10,... | collective-permute-start | bytes 1572872 | tf_op jit(solution)/shard_map/ppermute | solution.py:376
  214.5 37.3 %collective-permute-start.14 = (f32[8,64,256]{2,1,0:T(8,128)}, f32[8,64,256]{2,1,0:T(8,128)S(1)}, u32[]{:S(2)}, u32[]{:S(2)}) collective-permute-start(f32[8,64,256]{2,1,0:T(8,128)} %get-tuple-element.46), channel_id=1, source_target_pairs={{0,3},{1,2},{2,1},{3,0},{4,7},{5,6},{6,5},{7,4},{8,11},{9,10},{10,... | collective-permute-start | bytes 1572872 | tf_op jit(solution)/shard_map/ppermute | solution.py:376
  240.3 12.9 %copy-start.1 = (f32[8,64,256]{2,1,0:T(8,128)S(1)}, f32[8,64,256]{2,1,0:T(8,128)}, u32[]{:S(2)}) copy-start(f32[8,64,256]{2,1,0:T(8,128)} %get-tuple-element.38.refs_0_) | copy-start | bytes 1572868
  240.3 31.9 %collective-permute-start.8 = (f32[8,64,256]{2,1,0:T(8,128)}, f32[8,64,256]{2,1,0:T(8,128)}, u32[]{:S(2)}, u32[]{:S(2)}) collective-permute-start(f32[8,64,256]{2,1,0:T(8,128)} %get-tuple-element.37), channel_id=1, source_target_pairs={{0,1},{1,0},{2,3},{3,2},{4,5},{5,4},{6,7},{7,6},{8,9},{9,8},{10,11... | collective-permute-start | bytes 1572872 | tf_op jit(solution)/shard_map/ppermute | solution.py:376
  241.4 32.7 %collective-permute-start.7 = (f32[8,64,256]{2,1,0:T(8,128)}, f32[8,64,256]{2,1,0:T(8,128)S(1)}, u32[]{:S(2)}, u32[]{:S(2)}) collective-permute-start(f32[8,64,256]{2,1,0:T(8,128)} %get-tuple-element.36), channel_id=1, source_target_pairs={{0,3},{1,2},{2,1},{3,0},{4,7},{5,6},{6,5},{7,4},{8,11},{9,10},{10,... | collective-permute-start | bytes 1572872 | tf_op jit(solution)/shard_map/ppermute | solution.py:376
  243.8 62.0 %collective-permute-start.6 = (f32[8,64,256]{2,1,0:T(8,128)}, f32[8,64,256]{2,1,0:T(8,128)}, u32[]{:S(2)}, u32[]{:S(2)}) collective-permute-start(f32[8,64,256]{2,1,0:T(8,128)} %get-tuple-element.35), channel_id=1, source_target_pairs={{0,2},{1,3},{2,0},{3,1},{4,6},{5,7},{6,4},{7,5},{8,10},{9,11},{10,... | collective-permute-start | bytes 1572872 | tf_op jit(solution)/shard_map/ppermute | solution.py:376
where the time goes:
time: 308 us
  waiting for transfers between devices  185 us (60%)
  Pallas kernels  74.7 us (24%)
  starting transfers between devices  34.5 us (11%)
  blocking collectives  9.68 us (3%)
    ppermute x15, waiting for transfers between devices, swap(): lax.ppermute(arrays[step], 'depth', [(part, part ^ step) for part in rang...  146 us
    pallas_call x2, Pallas kernels, refocus(): pl.pallas_call(functools.partial(refocus_kernel, pieces), grid=(slots //...  48.7 us
    all_to_all x1, waiting for transfers between devices, exchange(): return lax.all_to_all(values, axes, split_axis=0, concat_axis=0, tiled=True)  39.6 us
    ppermute x15, starting transfers between devices, swap(): lax.ppermute(arrays[step], 'depth', [(part, part ^ step) for part in rang...  30 us
    all_to_all x1, blocking collectives, exchange(): return lax.all_to_all(values, axes, split_axis=0, concat_axis=0, tiled=True)  9.68 us
    pallas_call x2, Pallas kernels, in_order(): pl.pallas_call(functools.partial(order_kernel, chunk, chunks), in_specs=[...  6.86 us
    pallas_call x5, Pallas kernels, store(): pl.pallas_call(functools.partial(store_kernel, chunk, chunks, steps), in_...  6.65 us
  transfers between devices with their start and end apart: 16, of which 6 were waited for; matrix products, arithmetic and copies ran while one was open for 0% of the time, Pallas kernels for 21%

commit v1 on v0

--- a/solution.py
+++ b/solution.py
@@ -341,12 +341,13 @@
     )(slots, source)
 
 
-def store_kernel(chunk, chunks, steps, *refs):
+def store_kernel(chunk, chunks, steps, offset, *refs):
     source_refs, out_ref, gone = refs[: len(steps)], refs[-2], refs[-1]
 
     def copy(at, step):
         size = source_refs[at].shape[0]
-        first = pl.multiple_of((partner(step) * chunks + chunk) * size, size)
+        share = out_ref.shape[0] // (lax.axis_size("depth") * chunks)
+        first = (partner(step) * chunks + chunk) * share + offset
         return pltpu.make_async_copy(source_refs[at], out_ref.at[pl.ds(first, size)], gone.at[at])
 
     for at, step in enumerate(steps):
@@ -355,11 +356,11 @@
         copy(at, step).wait()
 
 
-def store(sources, into, out_shape, chunk, chunks, steps):
+def store(sources, into, out_shape, chunk, chunks, steps, offset=0):
     sources = [pltpu.with_memory_space_constraint(source, pltpu.VMEM) for source in sources]
     operands = sources if into is None else sources + [into]
     return pl.pallas_call(
-        functools.partial(store_kernel, chunk, chunks, steps),
+        functools.partial(store_kernel, chunk, chunks, steps, offset),
         in_specs=[LOCAL] * len(sources) + [ANYWHERE] * (into is not None),
         out_specs=ANYWHERE,
         out_shape=jax.ShapeDtypeStruct(out_shape, jnp.float32),
@@ -369,13 +370,17 @@
     )(*operands)
 
 
-def swap(arrays):
+def swap(arrays, halves=False):
     parts = len(arrays)
     swapped = list(arrays)
     for step in range(parts - 1, 0, -1):
-        swapped[step] = lax.ppermute(
-            arrays[step], "depth", [(part, part ^ step) for part in range(parts)]
-        )
+        pairs = [(part, part ^ step) for part in range(parts)]
+        if halves and step == 2:
+            swapped[step] = [
+                lax.ppermute(half, "depth", pairs) for half in jnp.split(arrays[step], 2)
+            ]
+        else:
+            swapped[step] = lax.ppermute(arrays[step], "depth", pairs)
     return swapped
 
 
@@ -398,12 +403,17 @@
         chosen = in_order(slots, arrived, parts, chunk, CHUNKS)
         chosen = swap(chosen)
         local = refocus(fields, chosen, chunk)
-        backs = swap(local)
+        backs = swap(local, chunk == CHUNKS - 1)
         every = tuple(range(parts))
         last = chunk == CHUNKS - 1
-        for steps in [(step,) for step in (*every[:2], *every[:1:-1])] if last else (every,):
-            sources = [backs[step] for step in steps]
-            result = store(sources, result, patches.shape, chunk, CHUNKS, steps)
+        if not last:
+            result = store(backs, result, patches.shape, chunk, CHUNKS, every)
+            continue
+        for step in (*every[:2], *every[:1:-1]):
+            first = 0
+            for source in jax.tree.leaves(backs[step]):
+                result = store([source], result, patches.shape, chunk, CHUNKS, (step,), first)
+                first += source.shape[0]
     return result
 
 

time: 308 us -> 308 us (level)
    ppermute x15 -> x16, waiting for transfers between devices: 146 us -> 142 us  [the longest x14 112 us: swap(): swapped[step] = lax.ppermute(arrays[step], 'depth', pairs)]
    pallas_call x5 -> x6, Pallas kernels: 6.65 us -> 7.19 us  [store(): pl.pallas_call(functools.partial(store_kernel, chunk, chunks, steps, offs...]
    ppermute x15 -> x16, starting transfers between devices: 30 us -> 30.1 us  [the longest x14 30 us: swap(): swapped[step] = lax.ppermute(arrays[step], 'depth', pairs)]
  transfers between devices with their start and end apart: 16 -> 17, of which waited for: 6 -> 7; matrix products, arithmetic and copies ran while one was open for 0% -> 1% of each run, Pallas kernels for 21% -> 22%
where the time goes in v1:
time: 308 us; the launch traced here: 307 us
  waiting for transfers between devices  182 us (59%)
  Pallas kernels  75.3 us (24%)
  starting transfers between devices  34.7 us (11%)
  blocking collectives  9.68 us (3%)
  local copies, waits for them, and re-layouts  4.6 us (1%)
    ppermute x14, waiting for transfers between devices, swap(): swapped[step] = lax.ppermute(arrays[step], 'depth', pairs)  112 us
    pallas_call x2, Pallas kernels, refocus(): pl.pallas_call(functools.partial(refocus_kernel, pieces), grid=(slots //...  48.7 us
    all_to_all x1, waiting for transfers between devices, exchange(): return lax.all_to_all(values, axes, split_axis=0, concat_axis=0, tiled=True)  39.6 us
    ppermute x2, waiting for transfers between devices, swap(): lax.ppermute(half, 'depth', pairs)  30.2 us
    ppermute x14, starting transfers between devices, swap(): swapped[step] = lax.ppermute(arrays[step], 'depth', pairs)  30 us
    all_to_all x1, blocking collectives, exchange(): return lax.all_to_all(values, axes, split_axis=0, concat_axis=0, tiled=True)  9.68 us
    pallas_call x6, Pallas kernels, store(): pl.pallas_call(functools.partial(store_kernel, chunk, chunks, steps, offs...  7.19 us
    pallas_call x2, Pallas kernels, in_order(): pl.pallas_call(functools.partial(order_kernel, chunk, chunks), in_specs=[...  6.88 us
  transfers between devices with their start and end apart: 17, of which 7 were waited for; matrix products, arithmetic and copies ran while one was open for 1% of the time, Pallas kernels for 22%

profile of v1, /device:TPU:0, one launch (start us, length us, event | category | flops | bytes accessed | tf_op | source)
XLA Modules:
  0.0 306.8 jit_solution(9978240404022460051)
XLA Ops:
  0.0 1.8 slot_table.1
  1.8 0.7 all_to_all.9
  2.5 9.7 %all_to_all.14 = s32[8,1,8]{2,1,0:T(1,128)S(1)} all-to-all(s32[8,1,8]{2,1,0:T(1,128)S(1)} %bitcast.4), channel_id=1, replica_groups=mesh['tile'=8,'depth'=4] {'tile'}, dimensions={0} | all-to-all | bytes 512 | tf_op jit(solution)/shard_map/all_to_all | solution.py:388
  12.2 0.5 broadcast.3
  12.7 0.7 reduce.3
  13.4 0.7 reshape.8.refs_0_
  14.1 5.8 %gather_blocks.1 = f32[64,64,256]{2,1,0:T(8,128)} custom-call(s32[64]{0:T(128)} %reshape.8.refs_0_, f32[64,64,256]{2,1,0:T(8,128)} %bitcast.3), custom_call_target="tpu_custom_call" | custom-call | tf_op jit(solution)/shard_map/gather_blocks/pallas_call | solution.py:196
  19.9 4.6 %all-to-all-start.1 = ((f32[64,64,256]{2,1,0:T(8,128)}), f32[64,64,256]{2,1,0:T(8,128)}, u32[]{:S(2)}, u32[]{:S(2)}) async-start(f32[64,64,256]{2,1,0:T(8,128)} %gather_blocks.1), calls=%async_computation.1 | async-start | bytes 8388608 | tf_op jit(solution)/shard_map/all_to_all | solution.py:388
  24.5 1.2 pieces.3
  25.7 3.7 %collective-permute-start.2 = (f32[16,64,256]{2,1,0:T(8,128)S(1)}, f32[16,64,256]{2,1,0:T(8,128)S(1)}, u32[]{:S(2)}, u32[]{:S(2)}) collective-permute-start(f32[16,64,256]{2,1,0:T(8,128)S(1)} %pieces.3), channel_id=1, source_target_pairs={{0,3},{1,2},{2,1},{3,0},{4,7},{5,6},{6,5},{7,4},{8,11},{9,10},{10,... | collective-permute-start | bytes 3145736 | tf_op jit(solution)/shard_map/ppermute | solution.py:383
  29.4 3.7 %pieces.2 = (f32[16,64,256]{2,1,0:T(8,128)}, f32[16,64,256]{2,1,0:T(8,128)}, f32[16,64,256]{2,1,0:T(8,128)}) custom-call(f32[64,64,256]{2,1,0:T(8,128)} %patches_ref.3), custom_call_target="tpu_custom_call" | custom-call | tf_op jit(solution)/shard_map/pieces/pallas_call | solution.py:246
  33.1 0.1 collective-permute-start
  33.2 0.8 collective-permute-start.1
  33.9 39.6 %all-to-all-done.1.source_ref = f32[64,64,256]{2,1,0:T(8,128)} async-done(((f32[64,64,256]{2,1,0:T(8,128)}), f32[64,64,256]{2,1,0:T(8,128)}, u32[]{:S(2)}, u32[]{:S(2)}) %all-to-all-start.1) | async-done | bytes 4194336 | tf_op jit(solution)/shard_map/all_to_all | solution.py:388
  73.6 3.4 %in_order.3 = (f32[8,64,256]{2,1,0:T(8,128)}, f32[8,64,256]{2,1,0:T(8,128)}, f32[8,64,256]{2,1,0:T(8,128)}, f32[8,64,256]{2,1,0:T(8,128)}) custom-call(s32[64]{0:T(128)} %get-tuple-element.29.slot_ref, f32[64,64,256]{2,1,0:T(8,128)} %all-to-all-done.1.source_ref), custom_call_target="tpu_custom_call" | custom-call | tf_op jit(solution)/shard_map/in_order/pallas_call | solution.py:330
  77.0 1.6 collective-permute-start.10
  78.6 2.6 collective-permute-start.11
  81.2 0.0 collective-permute-done.2.refs_3_
  81.2 0.2 collective-permute-start.12
  81.5 3.4 %in_order.2 = (f32[8,64,256]{2,1,0:T(8,128)}, f32[8,64,256]{2,1,0:T(8,128)}, f32[8,64,256]{2,1,0:T(8,128)}, f32[8,64,256]{2,1,0:T(8,128)}) custom-call(s32[64]{0:T(128)} %get-tuple-element.29.slot_ref, f32[64,64,256]{2,1,0:T(8,128)} %all-to-all-done.1.source_ref), custom_call_target="tpu_custom_call" | custom-call | tf_op jit(solution)/shard_map/in_order/pallas_call | solution.py:330
  84.9 0.0 copy-start.3
  84.9 0.7 collective-permute-start.3
  85.7 57.2 %collective-permute-done.1.refs_2_ = f32[16,64,256]{2,1,0:T(8,128)} collective-permute-done((f32[16,64,256]{2,1,0:T(8,128)}, f32[16,64,256]{2,1,0:T(8,128)}, u32[]{:S(2)}, u32[]{:S(2)}) %collective-permute-start.1) | collective-permute-done | bytes 1048608 | tf_op jit(solution)/shard_map/ppermute | solution.py:383
  142.9 2.5 collective-permute-start.5
  145.3 31.2 %collective-permute-done.11.refs_6_ = f32[8,64,256]{2,1,0:T(8,128)} collective-permute-done((f32[8,64,256]{2,1,0:T(8,128)}, f32[8,64,256]{2,1,0:T(8,128)}, u32[]{:S(2)}, u32[]{:S(2)}) %collective-permute-start.11) | collective-permute-done | bytes 524320 | tf_op jit(solution)/shard_map/ppermute | solution.py:383
  176.6 0.0 collective-permute-done.12.refs_7_
  176.6 24.3 %refocus.3 = (f32[8,64,256]{2,1,0:T(8,128)}, f32[8,64,256]{2,1,0:T(8,128)}, f32[8,64,256]{2,1,0:T(8,128)}, f32[8,64,256]{2,1,0:T(8,128)}) custom-call(bf16[4,256,256]{2,1,0:T(8,128)(2,1)} %constant.2.clone.table_ref, f32[16,64,256]{2,1,0:T(8,128)} %get-tuple-element.26.refs_0_, f32[16,64,256]{2,1,0:T(8,128)} %copy-done.3, ...), custom_call_target="tpu_custom_call" | custom-call | tf_op jit(solution)/shard_map/refocus/pallas_call | solution.py:145
  200.9 11.9 %collective-permute-start.13 = (f32[8,64,256]{2,1,0:T(8,128)}, f32[8,64,256]{2,1,0:T(8,128)S(1)}, u32[]{:S(2)}, u32[]{:S(2)}) collective-permute-start(f32[8,64,256]{2,1,0:T(8,128)} %get-tuple-element.44), channel_id=1, source_target_pairs={{0,1},{1,0},{2,3},{3,2},{4,5},{5,4},{6,7},{7,6},{8,9},{9,8},{10,11... | collective-permute-start | bytes 1572872 | tf_op jit(solution)/shard_map/ppermute | solution.py:383
  212.8 1.1 collective-permute-start.14
  213.9 1.5 collective-permute-start.15
  215.3 0.0 collective-permute-done.5.refs_7_
  215.3 0.8 copy-done.5
  216.1 24.3 %refocus.2 = (f32[8,64,256]{2,1,0:T(8,128)}, f32[8,64,256]{2,1,0:T(8,128)}, f32[8,64,256]{2,1,0:T(8,128)}, f32[8,64,256]{2,1,0:T(8,128)}) custom-call(bf16[4,256,256]{2,1,0:T(8,128)(2,1)} %constant.2.clone.table_ref, f32[16,64,256]{2,1,0:T(8,128)} %get-tuple-element.26.refs_0_, f32[16,64,256]{2,1,0:T(8,128)} %copy-done.3, ...), custom_call_target="tpu_custom_call" | custom-call | tf_op jit(solution)/shard_map/refocus/pallas_call | solution.py:145
  240.5 1.0 collective-permute-start.9
  241.5 2.5 collective-permute-start.8
  243.9 1.9 fusion
  245.8 0.1 collective-permute-start.7
  245.9 5.3 %collective-permute-done.14.refs_2_ = f32[8,64,256]{2,1,0:T(8,128)S(1)} collective-permute-done((f32[8,64,256]{2,1,0:T(8,128)}, f32[8,64,256]{2,1,0:T(8,128)S(1)}, u32[]{:S(2)}, u32[]{:S(2)}) %collective-permute-start.14) | collective-permute-done | bytes 524320 | tf_op jit(solution)/shard_map/ppermute | solution.py:383
  251.2 0.0 collective-permute-start.6
  251.2 1.4 store.6.refs_1_
  252.6 0.8 store.7.refs_1_
  253.4 18.2 %collective-permute-done.9.refs_0_ = f32[8,64,256]{2,1,0:T(8,128)} collective-permute-done((f32[8,64,256]{2,1,0:T(8,128)}, f32[8,64,256]{2,1,0:T(8,128)}, u32[]{:S(2)}, u32[]{:S(2)}) %collective-permute-start.9) | collective-permute-done | bytes 524320 | tf_op jit(solution)/shard_map/ppermute | solution.py:383
  271.6 1.8 store.8.refs_1_
  273.4 0.8 store.9.refs_1_
  274.3 27.5 %collective-permute-done.7.refs_0_ = f32[4,64,256]{2,1,0:T(8,128)S(1)} collective-permute-done((f32[4,64,256]{2,1,0:T(8,128)}, f32[4,64,256]{2,1,0:T(8,128)S(1)}, u32[]{:S(2)}, u32[]{:S(2)}) %collective-permute-start.7) | collective-permute-done | bytes 262176 | tf_op jit(solution)/shard_map/ppermute | solution.py:380
  301.8 0.7 store.10.refs_1_
  302.5 2.7 collective-permute-done.6.refs_0_
  305.2 1.7 store.11
  (18 shorter events, 0.0 us)
Async XLA Ops:
  19.9 53.7 %all-to-all-start.1 = ((f32[64,64,256]{2,1,0:T(8,128)}), f32[64,64,256]{2,1,0:T(8,128)}, u32[]{:S(2)}, u32[]{:S(2)}) async-start(f32[64,64,256]{2,1,0:T(8,128)} %gather_blocks.1), calls=%async_computation.1 | async-start | bytes 8388608 | tf_op jit(solution)/shard_map/all_to_all | solution.py:388
  25.7 55.5 %collective-permute-start.2 = (f32[16,64,256]{2,1,0:T(8,128)S(1)}, f32[16,64,256]{2,1,0:T(8,128)S(1)}, u32[]{:S(2)}, u32[]{:S(2)}) collective-permute-start(f32[16,64,256]{2,1,0:T(8,128)S(1)} %pieces.3), channel_id=1, source_target_pairs={{0,3},{1,2},{2,1},{3,0},{4,7},{5,6},{6,5},{7,4},{8,11},{9,10},{10,... | collective-permute-start | bytes 3145736 | tf_op jit(solution)/shard_map/ppermute | solution.py:383
  33.1 51.8 %collective-permute-start = (f32[16,64,256]{2,1,0:T(8,128)}, f32[16,64,256]{2,1,0:T(8,128)S(1)}, u32[]{:S(2)}, u32[]{:S(2)}) collective-permute-start(f32[16,64,256]{2,1,0:T(8,128)} %get-tuple-element.27), channel_id=1, source_target_pairs={{0,1},{1,0},{2,3},{3,2},{4,5},{5,4},{6,7},{7,6},{8,9},{9,8},{10,11... | collective-permute-start | bytes 3145736 | tf_op jit(solution)/shard_map/ppermute | solution.py:383
  33.2 109.7 %collective-permute-start.1 = (f32[16,64,256]{2,1,0:T(8,128)}, f32[16,64,256]{2,1,0:T(8,128)}, u32[]{:S(2)}, u32[]{:S(2)}) collective-permute-start(f32[16,64,256]{2,1,0:T(8,128)} %get-tuple-element.28), channel_id=1, source_target_pairs={{0,2},{1,3},{2,0},{3,1},{4,6},{5,7},{6,4},{7,5},{8,10},{9,11},{10,... | collective-permute-start | bytes 3145736 | tf_op jit(solution)/shard_map/ppermute | solution.py:383
  77.0 65.9 %collective-permute-start.10 = (f32[8,64,256]{2,1,0:T(8,128)}, f32[8,64,256]{2,1,0:T(8,128)}, u32[]{:S(2)}, u32[]{:S(2)}) collective-permute-start(f32[8,64,256]{2,1,0:T(8,128)} %get-tuple-element.40), channel_id=1, source_target_pairs={{0,1},{1,0},{2,3},{3,2},{4,5},{5,4},{6,7},{7,6},{8,9},{9,8},{10,11... | collective-permute-start | bytes 1572872 | tf_op jit(solution)/shard_map/ppermute | solution.py:383
  78.6 97.9 %collective-permute-start.11 = (f32[8,64,256]{2,1,0:T(8,128)}, f32[8,64,256]{2,1,0:T(8,128)}, u32[]{:S(2)}, u32[]{:S(2)}) collective-permute-start(f32[8,64,256]{2,1,0:T(8,128)} %get-tuple-element.41), channel_id=1, source_target_pairs={{0,2},{1,3},{2,0},{3,1},{4,6},{5,7},{6,4},{7,5},{8,10},{9,11},{10,... | collective-permute-start | bytes 1572872 | tf_op jit(solution)/shard_map/ppermute | solution.py:383
  81.2 95.3 %copy-start.2 = (f32[16,64,256]{2,1,0:T(8,128)}, f32[16,64,256]{2,1,0:T(8,128)S(1)}, u32[]{:S(2)}) copy-start(f32[16,64,256]{2,1,0:T(8,128)S(1)} %collective-permute-done.2.refs_3_) | copy-start | bytes 3145732
  81.2 95.3 %collective-permute-start.12 = (f32[8,64,256]{2,1,0:T(8,128)}, f32[8,64,256]{2,1,0:T(8,128)}, u32[]{:S(2)}, u32[]{:S(2)}) collective-permute-start(f32[8,64,256]{2,1,0:T(8,128)} %get-tuple-element.42), channel_id=1, source_target_pairs={{0,3},{1,2},{2,1},{3,0},{4,7},{5,6},{6,5},{7,4},{8,11},{9,10},{10,... | collective-permute-start | bytes 1572872 | tf_op jit(solution)/shard_map/ppermute | solution.py:383
  84.9 91.6 %copy-start.3 = (f32[16,64,256]{2,1,0:T(8,128)}, f32[16,64,256]{2,1,0:T(8,128)S(1)}, u32[]{:S(2)}) copy-start(f32[16,64,256]{2,1,0:T(8,128)S(1)} %collective-permute-done.refs_1_) | copy-start | bytes 3145732
  84.9 128.9 %collective-permute-start.3 = (f32[8,64,256]{2,1,0:T(8,128)}, f32[8,64,256]{2,1,0:T(8,128)S(1)}, u32[]{:S(2)}, u32[]{:S(2)}) collective-permute-start(f32[8,64,256]{2,1,0:T(8,128)} %get-tuple-element.32), channel_id=1, source_target_pairs={{0,1},{1,0},{2,3},{3,2},{4,5},{5,4},{6,7},{7,6},{8,9},{9,8},{10,11... | collective-permute-start | bytes 1572872 | tf_op jit(solution)/shard_map/ppermute | solution.py:383
  142.9 72.5 %collective-permute-start.4 = (f32[8,64,256]{2,1,0:T(8,128)}, f32[8,64,256]{2,1,0:T(8,128)S(1)}, u32[]{:S(2)}, u32[]{:S(2)}) collective-permute-start(f32[8,64,256]{2,1,0:T(8,128)} %get-tuple-element.33), channel_id=1, source_target_pairs={{0,2},{1,3},{2,0},{3,1},{4,6},{5,7},{6,4},{7,5},{8,10},{9,11},{10,... | collective-permute-start | bytes 1572872 | tf_op jit(solution)/shard_map/ppermute | solution.py:383
  142.9 72.5 %collective-permute-start.5 = (f32[8,64,256]{2,1,0:T(8,128)}, f32[8,64,256]{2,1,0:T(8,128)}, u32[]{:S(2)}, u32[]{:S(2)}) collective-permute-start(f32[8,64,256]{2,1,0:T(8,128)} %get-tuple-element.34), channel_id=1, source_target_pairs={{0,3},{1,2},{2,1},{3,0},{4,7},{5,6},{6,5},{7,4},{8,11},{9,10},{10,... | collective-permute-start | bytes 1572872 | tf_op jit(solution)/shard_map/ppermute | solution.py:383
  200.9 50.3 %copy-start = (f32[8,64,256]{2,1,0:T(8,128)S(1)}, f32[8,64,256]{2,1,0:T(8,128)}, u32[]{:S(2)}) copy-start(f32[8,64,256]{2,1,0:T(8,128)} %get-tuple-element.43.refs_0_) | copy-start | bytes 1572868
  200.9 44.9 %collective-permute-start.13 = (f32[8,64,256]{2,1,0:T(8,128)}, f32[8,64,256]{2,1,0:T(8,128)S(1)}, u32[]{:S(2)}, u32[]{:S(2)}) collective-permute-start(f32[8,64,256]{2,1,0:T(8,128)} %get-tuple-element.44), channel_id=1, source_target_pairs={{0,1},{1,0},{2,3},{3,2},{4,5},{5,4},{6,7},{7,6},{8,9},{9,8},{10,11... | collective-permute-start | bytes 1572872 | tf_op jit(solution)/shard_map/ppermute | solution.py:383
  212.8 38.4 %collective-permute-start.14 = (f32[8,64,256]{2,1,0:T(8,128)}, f32[8,64,256]{2,1,0:T(8,128)S(1)}, u32[]{:S(2)}, u32[]{:S(2)}) collective-permute-start(f32[8,64,256]{2,1,0:T(8,128)} %get-tuple-element.45), channel_id=1, source_target_pairs={{0,2},{1,3},{2,0},{3,1},{4,6},{5,7},{6,4},{7,5},{8,10},{9,11},{10,... | collective-permute-start | bytes 1572872 | tf_op jit(solution)/shard_map/ppermute | solution.py:383
  213.9 1.5 copy-start.4
  213.9 37.3 %collective-permute-start.15 = (f32[8,64,256]{2,1,0:T(8,128)}, f32[8,64,256]{2,1,0:T(8,128)S(1)}, u32[]{:S(2)}, u32[]{:S(2)}) collective-permute-start(f32[8,64,256]{2,1,0:T(8,128)} %get-tuple-element.46), channel_id=1, source_target_pairs={{0,3},{1,2},{2,1},{3,0},{4,7},{5,6},{6,5},{7,4},{8,11},{9,10},{10,... | collective-permute-start | bytes 1572872 | tf_op jit(solution)/shard_map/ppermute | solution.py:383
  215.3 0.8 copy-start.5
  240.4 12.1 %copy-start.1 = (f32[8,64,256]{2,1,0:T(8,128)S(1)}, f32[8,64,256]{2,1,0:T(8,128)}, u32[]{:S(2)}) copy-start(f32[8,64,256]{2,1,0:T(8,128)} %get-tuple-element.38.refs_0_) | copy-start | bytes 1572868
  240.5 31.1 %collective-permute-start.9 = (f32[8,64,256]{2,1,0:T(8,128)}, f32[8,64,256]{2,1,0:T(8,128)}, u32[]{:S(2)}, u32[]{:S(2)}) collective-permute-start(f32[8,64,256]{2,1,0:T(8,128)} %get-tuple-element.37), channel_id=1, source_target_pairs={{0,1},{1,0},{2,3},{3,2},{4,5},{5,4},{6,7},{7,6},{8,9},{9,8},{10,11... | collective-permute-start | bytes 1572872 | tf_op jit(solution)/shard_map/ppermute | solution.py:383
  241.5 31.9 %collective-permute-start.8 = (f32[8,64,256]{2,1,0:T(8,128)}, f32[8,64,256]{2,1,0:T(8,128)S(1)}, u32[]{:S(2)}, u32[]{:S(2)}) collective-permute-start(f32[8,64,256]{2,1,0:T(8,128)} %get-tuple-element.36), channel_id=1, source_target_pairs={{0,3},{1,2},{2,1},{3,0},{4,7},{5,6},{6,5},{7,4},{8,11},{9,10},{10,... | collective-permute-start | bytes 1572872 | tf_op jit(solution)/shard_map/ppermute | solution.py:383
  245.8 55.9 %collective-permute-start.7 = (f32[4,64,256]{2,1,0:T(8,128)}, f32[4,64,256]{2,1,0:T(8,128)S(1)}, u32[]{:S(2)}, u32[]{:S(2)}) collective-permute-start(f32[4,64,256]{2,1,0:T(8,128)} %get-tuple-element.47), channel_id=1, source_target_pairs={{0,2},{1,3},{2,0},{3,1},{4,6},{5,7},{6,4},{7,5},{8,10},{9,11},{10,... | collective-permute-start | bytes 786440 | tf_op jit(solution)/shard_map/ppermute | solution.py:380
  251.2 54.0 %collective-permute-start.6 = (f32[4,64,256]{2,1,0:T(8,128)}, f32[4,64,256]{2,1,0:T(8,128)}, u32[]{:S(2)}, u32[]{:S(2)}) collective-permute-start(f32[4,64,256]{2,1,0:T(8,128)} %get-tuple-element.48), channel_id=1, source_target_pairs={{0,2},{1,3},{2,0},{3,1},{4,6},{5,7},{6,4},{7,5},{8,10},{9,11},{10,... | collective-permute-start | bytes 786440 | tf_op jit(solution)/shard_map/ppermute | solution.py:380
